TPU v7x, 1024 devices: a whole 4x4x32 slice. The times are simulated.
1024 devices in a mesh: seq: 32 (over z_hi, x, y), ch: 32 (over z_lo, core).
Axes of the slice: x: 4, y: 4, z: 32 (z_hi: 2, z_lo: 16; z = z_hi * 16 + z_lo), core: 2. Of those that a mesh axis runs over, the one named last changes fastest.
Arguments:
- query: bfloat16 [4096, 8192], P('seq', 'ch'), may hold values from -6 to 6
- key_in: bfloat16 [4096, 8192], P('seq', 'ch'), may hold values from -6 to 6
- value: bfloat16 [4096, 8192], P('seq', 'ch'), may hold values from -6 to 6
- out_grad: bfloat16 [4096, 8192], P('seq', 'ch'), may hold values from -6 to 6
- filters: float32 [8192, 4096], P(('ch', 'seq')), may hold values from -6 to 6
Outputs:
- grad_query: bfloat16 [4096, 8192], P('seq', 'ch')
- grad_key: bfloat16 [4096, 8192], P('seq', 'ch')
- grad_value: bfloat16 [4096, 8192], P('seq', 'ch')
- filter_grad: float32 [8192, 4096], P(('ch', 'seq'))
All inputs are finite; a program needn't handle non-finite values.
Results may differ from a plain program's by a relative error of at most 0.0057.
Values may be sent and summed in bfloat16 or wider, within the bound.
No kernel may reach another device: no remote copies, remote signals or barrier semaphores. Data moves between devices by JAX's collectives and lax.ppermute only.
A program may use at most 32 MiB of HBM per device.

v0:
```python
import math

import jax
import jax.numpy as jnp
import numpy as np
from jax import lax
from jax.experimental import pallas as pl
from jax.experimental.pallas import tpu as pltpu
from jax.sharding import Mesh
from jax.sharding import PartitionSpec as P

BLK, CH, LANE = 16, 8, 128
ROWS = BLK * CH
HALF = BLK * LANE
f32, bf16 = jnp.float32, jnp.bfloat16


def split_terms(values):
    high = values.astype(np.float32).astype(bf16)
    low = (values - high.astype(np.float64)).astype(np.float32).astype(bf16)
    return high, low


def tables():
    odd = np.arange(BLK) + 0.5
    outer = 2 * np.pi * np.outer(odd, np.arange(BLK)) / (2 * BLK)
    eye = np.eye(CH)
    first = np.concatenate([np.kron(np.cos(outer), eye), np.kron(-np.sin(outer), eye)], 0)
    scale = 2.0 / (2 * HALF) / math.sqrt(2 * HALF)
    inner = 2 * np.pi * np.outer(np.arange(LANE), np.arange(LANE)) / LANE
    cosine, sine = np.cos(inner), np.sin(inner)
    wide = np.block([[cosine, -sine], [sine, cosine]])
    turn = 2 * np.pi * np.outer(odd, np.arange(LANE)) / (2 * HALF)
    turn = np.repeat(turn[:, None], CH, 1).reshape(ROWS, LANE)
    twiddle = np.stack([np.cos(turn), np.sin(turn)]).astype(np.float32)
    first_both = np.concatenate(split_terms(first), 1)
    wide_both = np.stack(split_terms(wide))
    back_both = np.stack(split_terms(wide.T))
    last_both = np.stack(split_terms(first.T * scale))
    return first_both, wide_both, back_both, last_both, twiddle


def dot(left, right):
    return jnp.dot(left, right, preferred_element_type=f32)


def terms(values):
    high = values.astype(bf16)
    return high, (values - high.astype(f32)).astype(bf16)


def spectra(signals, first, wide, twiddle):
    both = jnp.concatenate(signals, 1)
    part = dot(first[...], jnp.concatenate([both, both], 0))
    cosine, sine = twiddle[0], twiddle[1]
    turned = []
    for at in range(len(signals)):
        cols = slice(at * LANE, (at + 1) * LANE)
        real, imag = part[:ROWS, cols], part[ROWS:, cols]
        turned.append(
            jnp.concatenate([real * cosine + imag * sine, imag * cosine - real * sine], 1)
        )
    high, low = terms(jnp.concatenate(turned, 0))
    out = dot(high, wide[0]) + dot(low, wide[0]) + dot(high, wide[1])
    return [out[at * ROWS : (at + 1) * ROWS] for at in range(len(signals))]


def signals_of(spectrum_list, back, last, twiddle):
    high, low = terms(jnp.concatenate(spectrum_list, 0))
    inner = dot(high, back[0]) + dot(low, back[0]) + dot(high, back[1])
    cosine, sine = twiddle[0], twiddle[1]
    turned = []
    for at in range(len(spectrum_list)):
        rows = slice(at * ROWS, (at + 1) * ROWS)
        real, imag = inner[rows, :LANE], inner[rows, LANE:]
        turned.append(
            jnp.concatenate([real * cosine - imag * sine, real * sine + imag * cosine], 0)
        )
    high, low = terms(jnp.concatenate(turned, 1))
    out = dot(last[0], high) + dot(last[0], low) + dot(last[1], high)
    return [out[:, at * LANE : (at + 1) * LANE] for at in range(len(spectrum_list))]


def times(left, right):
    a, b, c, d = left[:, :LANE], left[:, LANE:], right[:, :LANE], right[:, LANE:]
    return jnp.concatenate([a * c - b * d, a * d + b * c], 1)


def times_conj(left, right, sign=1.0):
    a, b, c, d = left[:, :LANE], left[:, LANE:], right[:, :LANE], sign * right[:, LANE:]
    return jnp.concatenate([a * c + b * d, b * c - a * d], 1)


def alternate():
    k1 = lax.broadcasted_iota(jnp.int32, (ROWS, LANE), 0) // CH
    return (1 - 2 * (k1 % 2)).astype(f32)


def shifted(values, way):
    signs = way * alternate()
    return jnp.concatenate([signs * values[:, LANE:], -signs * values[:, :LANE]], 1)


def unpaired(pair):
    wide = pair.astype(f32)
    return (
        wide[:, :CH].reshape(ROWS, LANE),
        wide[:, CH:].reshape(ROWS, LANE),
    )


def paired(one, two):
    wide = jnp.concatenate([one.reshape(BLK, CH, LANE), two.reshape(BLK, CH, LANE)], 1)
    return wide.astype(bf16)


def gates_body(query, key_in, value, out_grad, sent):
    mixed = (key_in[...].astype(f32) * value[...].astype(f32)).astype(bf16).astype(f32)
    gated = (out_grad[...].astype(f32) * query[...].astype(f32)).astype(bf16).astype(f32)
    mixed = mixed.T.reshape(2, BLK, CH, LANE)
    gated = gated.T.reshape(2, BLK, CH, LANE)
    for half in range(2):
        sent[:, half] = jnp.concatenate([mixed[half], gated[half]], 1).astype(bf16)


def near_body(half, came, filters, first, wide, back, last, twiddle, own_spec, filt_spec, sent):
    side = half[0]
    flag = side.astype(f32)
    mix, gate = unpaired(came[:, side])
    filt = [filters[:, at * LANE : (at + 1) * LANE] for at in range(2 * BLK)]
    filt_lo = jnp.concatenate(filt[:BLK], 0)
    filt_hi = jnp.concatenate(filt[BLK:], 0)
    spec_mix, spec_gate, spec_lo, spec_hi = spectra(
        [mix.astype(bf16), gate.astype(bf16), filt_lo.astype(bf16), filt_hi.astype(bf16)],
        first,
        wide,
        twiddle,
    )
    cross = spec_hi + shifted(spec_lo, -1.0)
    chosen = spec_mix + flag * (spec_gate - spec_mix)
    far = signals_of(
        [times_conj(chosen, cross, 2.0 * flag - 1.0)], back, last, twiddle
    )[0]
    own_spec[0] = spec_mix
    own_spec[1] = spec_gate
    filt_spec[0] = spec_lo
    filt_spec[1] = cross
    sent[0] = came[:, 1 - side]
    sent[1] = paired(filt_lo, far)


def away_body(half, came, first, wide, twiddle, away_spec):
    mix, gate = unpaired(came[:, 1 - half[0]])
    spec_mix, spec_gate = spectra([mix.astype(bf16), gate.astype(bf16)], first, wide, twiddle)
    away_spec[0] = spec_mix
    away_spec[1] = spec_gate


def far_body(
    half, came, own_spec, filt_spec, away_spec, first, wide, back, last, twiddle, sent, filter_grad
):
    side = half[0]
    flag = side.astype(f32)
    mix, gate = unpaired(came[0])
    away_lo, away_far = unpaired(came[1])
    other_mix, other_gate, spec_away = spectra(
        [mix.astype(bf16), gate.astype(bf16), away_lo.astype(bf16)], first, wide, twiddle
    )
    own_mix, own_gate = own_spec[0], own_spec[1]
    spec_lo, cross = filt_spec[0], filt_spec[1]
    early_mix = own_mix + flag * (other_mix - own_mix)
    late_gate = other_gate + flag * (own_gate - other_gate)
    lag_cross = times_conj(late_gate, early_mix)
    lag_same = times_conj(own_gate, own_mix) + times_conj(other_gate, other_mix)
    chosen = other_gate + flag * (other_mix - other_gate)
    extra = times_conj(chosen, cross, 1.0 - 2.0 * flag)
    conv = times(own_mix, spec_lo) + flag * extra
    grad = times_conj(own_gate, spec_lo) + (1.0 - flag) * extra
    conv_away = times(away_spec[0], spec_away)
    grad_away = times_conj(away_spec[1], spec_away)
    conv, grad, conv_away, grad_away, lag_lo, lag_hi = signals_of(
        [conv, grad, conv_away, grad_away, lag_same + shifted(lag_cross, 1.0), lag_cross],
        back,
        last,
        twiddle,
    )
    sent[:, side] = paired(conv, grad)
    sent[:, 1 - side] = paired(
        conv_away + flag * away_far, grad_away + (1.0 - flag) * away_far
    )
    for at in range(BLK):
        rows = slice(at * CH, (at + 1) * CH)
        filter_grad[:, at * LANE : (at + 1) * LANE] = lag_lo[rows]
        filter_grad[:, HALF + at * LANE : HALF + (at + 1) * LANE] = lag_hi[rows]


def last_body(came, key_in, value, out_grad, grad_query, grad_key, grad_value):
    wide = came[...].astype(f32)
    conv = wide[:, :, :CH].transpose(1, 0, 2, 3).reshape(2 * ROWS, LANE).T
    grad = wide[:, :, CH:].transpose(1, 0, 2, 3).reshape(2 * ROWS, LANE).T
    grad_query[...] = (out_grad[...].astype(f32) * conv).astype(bf16)
    grad_key[...] = (grad * value[...].astype(f32)).astype(bf16)
    grad_value[...] = (grad * key_in[...].astype(f32)).astype(bf16)


def call(body, outs, *operands, scalar=False, name):
    specs = [pl.BlockSpec(memory_space=pltpu.VMEM) for _ in operands]
    if scalar:
        specs[0] = pl.BlockSpec(memory_space=pltpu.SMEM)
    return pl.pallas_call(
        body,
        out_shape=[jax.ShapeDtypeStruct(*out) for out in outs],
        in_specs=specs,
        out_specs=[pl.BlockSpec(memory_space=pltpu.VMEM) for _ in outs],
        name=name,
    )(*operands)


PAIR = ((BLK, 2, 2 * CH, LANE), bf16)


def swap_pieces(pieces):
    return lax.all_to_all(
        pieces.reshape(BLK, 4 * CH, LANE), ("x", "y"), split_axis=0, concat_axis=0, tiled=True
    ).reshape(PAIR[0])


def on_device(query, key_in, value, out_grad, filters):
    half = lax.axis_index("z_hi").reshape(1).astype(jnp.int32)
    first, wide, back, last, twiddle = (jnp.asarray(table) for table in tables())
    (sent,) = call(gates_body, [PAIR], query, key_in, value, out_grad, name="gates")
    came = swap_pieces(sent)
    spec = ((2, ROWS, 2 * LANE), f32)
    own_spec, filt_spec, sent = call(
        near_body,
        [spec, spec, ((2, BLK, 2 * CH, LANE), bf16)],
        half, came, filters, first, wide, back, last, twiddle,
        scalar=True, name="near",
    )
    crossed = lax.ppermute(sent, "z_hi", [(0, 1), (1, 0)])
    (away_spec,) = call(
        away_body, [spec], half, came, first, wide, twiddle, scalar=True, name="away"
    )
    sent, filter_grad = call(
        far_body,
        [PAIR, (filters.shape, f32)],
        half, crossed, own_spec, filt_spec, away_spec, first, wide, back, last, twiddle,
        scalar=True, name="far",
    )
    came = swap_pieces(sent)
    gate = (query.shape, bf16)
    grads = call(
        last_body, [gate] * 3, came, key_in, value, out_grad, name="last"
    )
    return (*grads, filter_grad)


def solution(mesh):
    axes = (2, 4, 4, 16, 2)
    fine = Mesh(mesh.devices.reshape(axes), ("z_hi", "x", "y", "z_lo", "core"))
    seq, ch = ("z_hi", "x", "y"), ("z_lo", "core")
    gate, filt = P(seq, ch), P(ch + seq, None)
    return jax.shard_map(
        on_device,
        mesh=fine,
        in_specs=(gate, gate, gate, gate, filt),
        out_specs=(gate, gate, gate, filt),
        check_vma=False,
    )
```

profile of v0, /device:TPU:32, one launch (start us, length us, event | category | flops | bytes accessed | tf_op | source)
XLA Modules:
  0.0 88.9 jit_solution(7492531328255921855)
XLA Ops:
  0.6 1.7 %gates.1 = bf16[16,2,16,128]{3,2,1,0:T(8,128)(2,1)} custom-call(bf16[128,256]{1,0:T(8,128)(2,1)} %query.1, bf16[128,256]{1,0:T(8,128)(2,1)} %key_in.3, bf16[128,256]{1,0:T(8,128)(2,1)} %value.3, bf16[128,256]{1,0:T(8,128)(2,1)} %out_grad.3), custom_call_target="tpu_custom_call" | custom-call | tf_op jit(solution)/shard_map/gates/pallas_call | solution.py:210
  2.3 7.0 %all-to-all-start = ((bf16[16,32,128]{2,1,0:T(8,128)(2,1)}), bf16[16,32,128]{2,1,0:T(8,128)(2,1)S(1)}, u32[]{:S(2)}, u32[]{:S(2)}) async-start(bf16[16,32,128]{2,1,0:T(8,128)(2,1)} %bitcast.7), calls=%async_computation | async-start | bytes 262144 | tf_op jit(solution)/shard_map/all_to_all | solution.py:223
  9.4 7.8 %all-to-all-done = bf16[16,32,128]{2,1,0:T(8,128)(2,1)S(1)} async-done(((bf16[16,32,128]{2,1,0:T(8,128)(2,1)}), bf16[16,32,128]{2,1,0:T(8,128)(2,1)S(1)}, u32[]{:S(2)}, u32[]{:S(2)}) %all-to-all-start) | async-done | bytes 131104 | tf_op jit(solution)/shard_map/all_to_all | solution.py:223
  17.2 0.0 copy-start
  17.2 0.7 copy-done
  17.9 3.0 %near.1 = (f32[2,128,256]{2,1,0:T(8,128)}, f32[2,128,256]{2,1,0:T(8,128)}, bf16[2,16,16,128]{3,2,1,0:T(8,128)(2,1)}) custom-call(s32[1]{0:T(128)} %bitcast.half, bf16[16,2,16,128]{3,2,1,0:T(8,128)(2,1)} %bitcast.5, f32[8,4096]{1,0:T(8,128)} %filters.1, bf16[256,256]{1,0:T(8,128)(2,1)} %constant.16.clone.first, bf16[2,256,256]{2,1,0:T(8,128)(2,1)} %constant.17.clone.wide, ...), custom_call_target="tpu_custom_call" | custom-call | tf_op jit(solution)/shard_map/near/pallas_call | solution.py:210
  20.9 28.1 %collective-permute-start = (bf16[2,16,16,128]{3,2,1,0:T(8,128)(2,1)}, bf16[2,16,16,128]{3,2,1,0:T(8,128)(2,1)S(1)}, u32[]{:S(2)}, u32[]{:S(2)}) collective-permute-start(bf16[2,16,16,128]{3,2,1,0:T(8,128)(2,1)} %get-tuple-element.12), channel_id=1, source_target_pairs={{0,512},{512,0},{1,513},{513,1},{2,514},{514,2},{3,515},{515,3},{4... | collective-permute-start | bytes 393224 | tf_op jit(solution)/shard_map/ppermute | solution.py:240
  49.0 2.3 %away.1.away_spec = f32[2,128,256]{2,1,0:T(8,128)} custom-call(s32[1]{0:T(128)} %bitcast.half, bf16[16,2,16,128]{3,2,1,0:T(8,128)(2,1)} %bitcast.6, bf16[256,256]{1,0:T(8,128)(2,1)} %constant.16.clone.first, bf16[2,256,256]{2,1,0:T(8,128)(2,1)} %constant.17.clone.wide, f32[2,128,128]{2,1,0:T(8,128)} %constant.20.clone.twiddle), custom_call_target="tpu_custom_call" | custom-call | tf_op jit(solution)/shard_map/away/pallas_call | solution.py:210
  51.2 19.5 %collective-permute-done.came = bf16[2,16,16,128]{3,2,1,0:T(8,128)(2,1)S(1)} collective-permute-done((bf16[2,16,16,128]{3,2,1,0:T(8,128)(2,1)}, bf16[2,16,16,128]{3,2,1,0:T(8,128)(2,1)S(1)}, u32[]{:S(2)}, u32[]{:S(2)}) %collective-permute-start) | collective-permute-done | bytes 131104 | tf_op jit(solution)/shard_map/ppermute | solution.py:240
  70.7 0.0 copy-start.1
  70.7 0.6 copy-done.1
  71.4 3.8 %far.1 = (bf16[16,2,16,128]{3,2,1,0:T(8,128)(2,1)}, f32[8,4096]{1,0:T(8,128)}) custom-call(s32[1]{0:T(128)} %bitcast.half, bf16[2,16,16,128]{3,2,1,0:T(8,128)(2,1)} %copy-done.1, f32[2,128,256]{2,1,0:T(8,128)} %get-tuple-element.13.own_spec, f32[2,128,256]{2,1,0:T(8,128)} %get-tuple-element.14.filt_spec, f32[2,128,256]{2,1,0:T(8,128)} %away.1.away_spec, ...), custom_call_target="tpu_custom_call" | custom-call | tf_op jit(solution)/shard_map/far/pallas_call | solution.py:210
  75.2 12.0 %all_to_all.10 = bf16[16,32,128]{2,1,0:T(8,128)(2,1)} all-to-all(bf16[16,32,128]{2,1,0:T(8,128)(2,1)} %bitcast.9), channel_id=1, replica_groups=mesh['z_hi'=2,'x'=4,'y'=4,'z_lo'=16,'core'=2] {'x','y'}, dimensions={0} | all-to-all | bytes 262144 | tf_op jit(solution)/shard_map/all_to_all | solution.py:223
  87.2 1.8 %last.3 = (bf16[128,256]{1,0:T(8,128)(2,1)}, bf16[128,256]{1,0:T(8,128)(2,1)}, bf16[128,256]{1,0:T(8,128)(2,1)}) custom-call(bf16[16,2,16,128]{3,2,1,0:T(8,128)(2,1)} %bitcast.8, bf16[128,256]{1,0:T(8,128)(2,1)} %key_in.3, bf16[128,256]{1,0:T(8,128)(2,1)} %value.3, bf16[128,256]{1,0:T(8,128)(2,1)} %out_grad.3), custom_call_target="tpu_custom_call" | custom-call | tf_op jit(solution)/shard_map/last/pallas_call | solution.py:210
Async XLA Ops:
  2.3 14.9 %all-to-all-start = ((bf16[16,32,128]{2,1,0:T(8,128)(2,1)}), bf16[16,32,128]{2,1,0:T(8,128)(2,1)S(1)}, u32[]{:S(2)}, u32[]{:S(2)}) async-start(bf16[16,32,128]{2,1,0:T(8,128)(2,1)} %bitcast.7), calls=%async_computation | async-start | bytes 262144 | tf_op jit(solution)/shard_map/all_to_all | solution.py:223
  17.2 0.7 copy-start
  20.9 49.8 %collective-permute-start = (bf16[2,16,16,128]{3,2,1,0:T(8,128)(2,1)}, bf16[2,16,16,128]{3,2,1,0:T(8,128)(2,1)S(1)}, u32[]{:S(2)}, u32[]{:S(2)}) collective-permute-start(bf16[2,16,16,128]{3,2,1,0:T(8,128)(2,1)} %get-tuple-element.12), channel_id=1, source_target_pairs={{0,512},{512,0},{1,513},{513,1},{2,514},{514,2},{3,515},{515,3},{4... | collective-permute-start | bytes 393224 | tf_op jit(solution)/shard_map/ppermute | solution.py:240
  70.7 0.6 copy-start.1
where the time goes:
time: 89.4 us; the launch traced here: 88.9 us
  starting transfers between devices  35.1 us (39%)
  waiting for transfers between devices  27.3 us (31%)
  Pallas kernels  12.6 us (14%)
  blocking collectives  12 us (13%)
  local copies, waits for them, and re-layouts  1.3 us (1%)
    ppermute x1, starting transfers between devices, on_device(): crossed = lax.ppermute(sent, 'z_hi', [(0, 1), (1, 0)])  28.1 us
    ppermute x1, waiting for transfers between devices, on_device(): crossed = lax.ppermute(sent, 'z_hi', [(0, 1), (1, 0)])  19.5 us
    pallas_call x5, Pallas kernels, call(): pl.pallas_call(body, out_shape=[jax.ShapeDtypeStruct(*out) for out in out...  12.6 us
    all_to_all x1, blocking collectives, swap_pieces(): lax.all_to_all(pieces.reshape(BLK, 4 * CH, LANE), ('x', 'y'), split_axis=...  12 us
    all_to_all x1, waiting for transfers between devices, swap_pieces(): lax.all_to_all(pieces.reshape(BLK, 4 * CH, LANE), ('x', 'y'), split_axis=...  7.84 us
    all_to_all x1, starting transfers between devices, swap_pieces(): lax.all_to_all(pieces.reshape(BLK, 4 * CH, LANE), ('x', 'y'), split_axis=...  7.03 us
  transfers between devices with their start and end apart: 2, of which 2 were waited for; matrix products, arithmetic and copies ran while one was open for 0% of the time, Pallas kernels for 3%

commit v1 on v0

--- a/solution.py
+++ b/solution.py
@@ -35,13 +35,16 @@
     twiddle = np.stack([np.cos(turn), np.sin(turn)]).astype(np.float32)
     first_both = np.concatenate(split_terms(first), 1)
     wide_both = np.stack(split_terms(wide))
-    back_both = np.stack(split_terms(wide.T))
     last_both = np.stack(split_terms(first.T * scale))
-    return first_both, wide_both, back_both, last_both, twiddle
+    return first_both, wide_both, last_both, twiddle
 
 
 def dot(left, right):
     return jnp.dot(left, right, preferred_element_type=f32)
+
+
+def dot_back(left, right):
+    return lax.dot_general(left, right, (((1,), (1,)), ((), ())), preferred_element_type=f32)
 
 
 def terms(values):
@@ -65,9 +68,9 @@
     return [out[at * ROWS : (at + 1) * ROWS] for at in range(len(signals))]
 
 
-def signals_of(spectrum_list, back, last, twiddle):
+def signals_of(spectrum_list, wide, last, twiddle):
     high, low = terms(jnp.concatenate(spectrum_list, 0))
-    inner = dot(high, back[0]) + dot(low, back[0]) + dot(high, back[1])
+    inner = dot_back(high, wide[0]) + dot_back(low, wide[0]) + dot_back(high, wide[1])
     cosine, sine = twiddle[0], twiddle[1]
     turned = []
     for at in range(len(spectrum_list)):
@@ -114,22 +117,22 @@
     return wide.astype(bf16)
 
 
-def gates_body(query, key_in, value, out_grad, sent):
+def gates_body(query, key_in, value, out_grad, filters, sent, filt_pair):
     mixed = (key_in[...].astype(f32) * value[...].astype(f32)).astype(bf16).astype(f32)
     gated = (out_grad[...].astype(f32) * query[...].astype(f32)).astype(bf16).astype(f32)
     mixed = mixed.T.reshape(2, BLK, CH, LANE)
     gated = gated.T.reshape(2, BLK, CH, LANE)
     for half in range(2):
         sent[:, half] = jnp.concatenate([mixed[half], gated[half]], 1).astype(bf16)
-
-
-def near_body(half, came, filters, first, wide, back, last, twiddle, own_spec, filt_spec, sent):
+    filt = [filters[:, at * LANE : (at + 1) * LANE] for at in range(2 * BLK)]
+    filt_pair[...] = paired(jnp.concatenate(filt[:BLK], 0), jnp.concatenate(filt[BLK:], 0))
+
+
+def near_body(half, came, filt_pair, first, wide, last, twiddle, own_spec, filt_spec, sent):
     side = half[0]
     flag = side.astype(f32)
     mix, gate = unpaired(came[:, side])
-    filt = [filters[:, at * LANE : (at + 1) * LANE] for at in range(2 * BLK)]
-    filt_lo = jnp.concatenate(filt[:BLK], 0)
-    filt_hi = jnp.concatenate(filt[BLK:], 0)
+    filt_lo, filt_hi = unpaired(filt_pair[...])
     spec_mix, spec_gate, spec_lo, spec_hi = spectra(
         [mix.astype(bf16), gate.astype(bf16), filt_lo.astype(bf16), filt_hi.astype(bf16)],
         first,
@@ -139,7 +142,7 @@
     cross = spec_hi + shifted(spec_lo, -1.0)
     chosen = spec_mix + flag * (spec_gate - spec_mix)
     far = signals_of(
-        [times_conj(chosen, cross, 2.0 * flag - 1.0)], back, last, twiddle
+        [times_conj(chosen, cross, 2.0 * flag - 1.0)], wide, last, twiddle
     )[0]
     own_spec[0] = spec_mix
     own_spec[1] = spec_gate
@@ -157,7 +160,7 @@
 
 
 def far_body(
-    half, came, own_spec, filt_spec, away_spec, first, wide, back, last, twiddle, sent, filter_grad
+    half, came, own_spec, filt_spec, away_spec, first, wide, last, twiddle, sent, filter_grad
 ):
     side = half[0]
     flag = side.astype(f32)
@@ -180,7 +183,7 @@
     grad_away = times_conj(away_spec[1], spec_away)
     conv, grad, conv_away, grad_away, lag_lo, lag_hi = signals_of(
         [conv, grad, conv_away, grad_away, lag_same + shifted(lag_cross, 1.0), lag_cross],
-        back,
+        wide,
         last,
         twiddle,
     )
@@ -203,13 +206,20 @@
     grad_value[...] = (grad * key_in[...].astype(f32)).astype(bf16)
 
 
-def call(body, outs, *operands, scalar=False, name):
+def near_memory(array):
+    return pltpu.with_memory_space_constraint(array, pltpu.VMEM)
+
+
+def call(body, outs, *operands, scalar=False, far_in=False, far_out=False, name):
     specs = [pl.BlockSpec(memory_space=pltpu.VMEM) for _ in operands]
     if scalar:
         specs[0] = pl.BlockSpec(memory_space=pltpu.SMEM)
+    if not far_in:
+        operands = (*operands[:scalar], *map(near_memory, operands[scalar:]))
+    kind = jax.ShapeDtypeStruct if far_out else pltpu.VMEM
     return pl.pallas_call(
         body,
-        out_shape=[jax.ShapeDtypeStruct(*out) for out in outs],
+        out_shape=[kind(*out) for out in outs],
         in_specs=specs,
         out_specs=[pl.BlockSpec(memory_space=pltpu.VMEM) for _ in outs],
         name=name,
@@ -217,6 +227,7 @@
 
 
 PAIR = ((BLK, 2, 2 * CH, LANE), bf16)
+ONE = ((BLK, 2 * CH, LANE), bf16)
 
 
 def swap_pieces(pieces):
@@ -227,14 +238,16 @@
 
 def on_device(query, key_in, value, out_grad, filters):
     half = lax.axis_index("z_hi").reshape(1).astype(jnp.int32)
-    first, wide, back, last, twiddle = (jnp.asarray(table) for table in tables())
-    (sent,) = call(gates_body, [PAIR], query, key_in, value, out_grad, name="gates")
+    first, wide, last, twiddle = (jnp.asarray(table) for table in tables())
+    sent, filt_pair = call(
+        gates_body, [PAIR, ONE], query, key_in, value, out_grad, filters, far_in=True, name="gates"
+    )
     came = swap_pieces(sent)
     spec = ((2, ROWS, 2 * LANE), f32)
     own_spec, filt_spec, sent = call(
         near_body,
         [spec, spec, ((2, BLK, 2 * CH, LANE), bf16)],
-        half, came, filters, first, wide, back, last, twiddle,
+        half, came, filt_pair, first, wide, last, twiddle,
         scalar=True, name="near",
     )
     crossed = lax.ppermute(sent, "z_hi", [(0, 1), (1, 0)])
@@ -244,13 +257,13 @@
     sent, filter_grad = call(
         far_body,
         [PAIR, (filters.shape, f32)],
-        half, crossed, own_spec, filt_spec, away_spec, first, wide, back, last, twiddle,
+        half, crossed, own_spec, filt_spec, away_spec, first, wide, last, twiddle,
         scalar=True, name="far",
     )
     came = swap_pieces(sent)
     gate = (query.shape, bf16)
     grads = call(
-        last_body, [gate] * 3, came, key_in, value, out_grad, name="last"
+        last_body, [gate] * 3, came, key_in, value, out_grad, far_out=True, name="last"
     )
     return (*grads, filter_grad)
 

time: 89.4 us -> 83.6 us (0.935)
  blocking collectives: 12 us -> 0 us
  waiting for transfers between devices: 27.3 us -> 36 us
  Pallas kernels: 12.6 us -> 6.71 us
  starting transfers between devices: 35.1 us -> 39.1 us
    all_to_all x1 -> x0, blocking collectives: 12 us -> none  [swap_pieces(): lax.all_to_all(pieces.reshape(BLK, 4 * CH, LANE), ('x', 'y'), split_axis=...]
    all_to_all x1 -> x2, waiting for transfers between devices: 7.84 us -> 15 us  [swap_pieces(): lax.all_to_all(pieces.reshape(BLK, 4 * CH, LANE), ('x', 'y'), split_axis=...]
    pallas_call x5, Pallas kernels: 12.6 us -> 6.71 us  [call(): pl.pallas_call(body, out_shape=[kind(*out) for out in outs], in_specs=spe...]
    all_to_all x1 -> x2, starting transfers between devices: 7.03 us -> 11 us  [swap_pieces(): lax.all_to_all(pieces.reshape(BLK, 4 * CH, LANE), ('x', 'y'), split_axis=...]
    ppermute x1, waiting for transfers between devices: 19.5 us -> 21.1 us  [on_device(): crossed = lax.ppermute(sent, 'z_hi', [(0, 1), (1, 0)])]
  transfers between devices with their start and end apart: 2 -> 3, of which waited for: 2 -> 3; matrix products, arithmetic and copies ran while one was open for 0% -> 1% of each run, Pallas kernels for 3% -> 1%
where the time goes in v1:
time: 83.6 us; the launch traced here: 83.3 us
  starting transfers between devices  39.1 us (47%)
  waiting for transfers between devices  36 us (43%)
  Pallas kernels  6.71 us (8%)
    ppermute x1, starting transfers between devices, on_device(): crossed = lax.ppermute(sent, 'z_hi', [(0, 1), (1, 0)])  28.1 us
    ppermute x1, waiting for transfers between devices, on_device(): crossed = lax.ppermute(sent, 'z_hi', [(0, 1), (1, 0)])  21.1 us
    all_to_all x2, waiting for transfers between devices, swap_pieces(): lax.all_to_all(pieces.reshape(BLK, 4 * CH, LANE), ('x', 'y'), split_axis=...  15 us
    all_to_all x2, starting transfers between devices, swap_pieces(): lax.all_to_all(pieces.reshape(BLK, 4 * CH, LANE), ('x', 'y'), split_axis=...  11 us
    pallas_call x5, Pallas kernels, call(): pl.pallas_call(body, out_shape=[kind(*out) for out in outs], in_specs=spe...  6.71 us
  transfers between devices with their start and end apart: 3, of which 3 were waited for; matrix products, arithmetic and copies ran while one was open for 1% of the time, Pallas kernels for 1%

profile of v1, /device:TPU:32, one launch (start us, length us, event | category | flops | bytes accessed | tf_op | source)
XLA Modules:
  0.0 83.3 jit_solution(16055892229410696420)
XLA Ops:
  0.6 0.0 copy-start
  0.6 0.0 copy-start.3
  0.7 1.8 %gates.1 = (bf16[16,2,16,128]{3,2,1,0:T(8,128)(2,1)}, bf16[16,16,128]{2,1,0:T(8,128)(2,1)S(1)}) custom-call(bf16[128,256]{1,0:T(8,128)(2,1)} %query.1, bf16[128,256]{1,0:T(8,128)(2,1)} %key_in.3, bf16[128,256]{1,0:T(8,128)(2,1)} %value.3, bf16[128,256]{1,0:T(8,128)(2,1)} %out_grad.3, f32[8,4096]{1,0:T(8,128)} %filters.1), custom_call_target="tpu_custom_call" | custom-call | tf_op jit(solution)/shard_map/gates/pallas_call | solution.py:220
  2.5 7.2 %all-to-all-start = ((bf16[16,32,128]{2,1,0:T(8,128)(2,1)}), bf16[16,32,128]{2,1,0:T(8,128)(2,1)S(1)}, u32[]{:S(2)}, u32[]{:S(2)}) async-start(bf16[16,32,128]{2,1,0:T(8,128)(2,1)} %bitcast.1), calls=%async_computation | async-start | bytes 262144 | tf_op jit(solution)/shard_map/all_to_all | solution.py:234
  9.7 7.8 %all-to-all-done = bf16[16,32,128]{2,1,0:T(8,128)(2,1)S(1)} async-done(((bf16[16,32,128]{2,1,0:T(8,128)(2,1)}), bf16[16,32,128]{2,1,0:T(8,128)(2,1)S(1)}, u32[]{:S(2)}, u32[]{:S(2)}) %all-to-all-start) | async-done | bytes 131104 | tf_op jit(solution)/shard_map/all_to_all | solution.py:234
  17.5 0.0 copy-done
  17.5 0.0 copy-done.3
  17.5 0.0 copy-done.1
  17.5 0.0 copy-done.2
  17.5 1.2 %near.1 = (f32[2,128,256]{2,1,0:T(8,128)S(1)}, f32[2,128,256]{2,1,0:T(8,128)S(1)}, bf16[2,16,16,128]{3,2,1,0:T(8,128)(2,1)S(1)}) custom-call(s32[1]{0:T(128)} %bitcast.half, bf16[16,2,16,128]{3,2,1,0:T(8,128)(2,1)S(1)} %bitcast.5, bf16[16,16,128]{2,1,0:T(8,128)(2,1)S(1)} %get-tuple-element.15.filt_pair, bf16[256,256]{1,0:T(8,128)(2,1)S(1)} %copy-done.2, ...), custom_call_target="tpu_custom_call" | custom-call | tf_op jit(solution)/shard_map/near/pallas_call | solution.py:220
  18.8 28.1 %collective-permute-start = (bf16[2,16,16,128]{3,2,1,0:T(8,128)(2,1)S(1)}, bf16[2,16,16,128]{3,2,1,0:T(8,128)(2,1)S(1)}, u32[]{:S(2)}, u32[]{:S(2)}) collective-permute-start(bf16[2,16,16,128]{3,2,1,0:T(8,128)(2,1)S(1)} %get-tuple-element.16), channel_id=1, source_target_pairs={{0,512},{512,0},{1,513},{513,1},{2,514},{514,2},{3,515},{515,3},{4... | collective-permute-start | bytes 393224 | tf_op jit(solution)/shard_map/ppermute | solution.py:253
  46.9 0.5 away.1.away_spec
  47.3 21.1 %collective-permute-done.came = bf16[2,16,16,128]{3,2,1,0:T(8,128)(2,1)S(1)} collective-permute-done((bf16[2,16,16,128]{3,2,1,0:T(8,128)(2,1)S(1)}, bf16[2,16,16,128]{3,2,1,0:T(8,128)(2,1)S(1)}, u32[]{:S(2)}, u32[]{:S(2)}) %collective-permute-start) | collective-permute-done | bytes 131104 | tf_op jit(solution)/shard_map/ppermute | solution.py:253
  68.4 2.4 %far.1 = (bf16[16,2,16,128]{3,2,1,0:T(8,128)(2,1)}, f32[8,4096]{1,0:T(8,128)S(1)}) custom-call(s32[1]{0:T(128)} %bitcast.half, bf16[2,16,16,128]{3,2,1,0:T(8,128)(2,1)S(1)} %collective-permute-done.came, f32[2,128,256]{2,1,0:T(8,128)S(1)} %get-tuple-element.17.own_spec, f32[2,128,256]{2,1,0:T(8,128)S(1)} %get-tuple-element.18.filt_spec, ...), custom_call_target="tpu_custom_call" | custom-call | tf_op jit(solution)/shard_map/far/pallas_call | solution.py:220
  70.8 3.8 %all-to-all-start.1 = ((bf16[16,32,128]{2,1,0:T(8,128)(2,1)}), bf16[16,32,128]{2,1,0:T(8,128)(2,1)S(1)}, u32[]{:S(2)}, u32[]{:S(2)}) async-start(bf16[16,32,128]{2,1,0:T(8,128)(2,1)} %bitcast.3), calls=%async_computation.1 | async-start | bytes 262144 | tf_op jit(solution)/shard_map/all_to_all | solution.py:234
  74.6 0.0 copy-start.4
  74.6 0.0 copy-start.5
  74.6 0.0 copy-start.6
  74.7 0.7 copy.13
  75.3 7.1 %all-to-all-done.1 = bf16[16,32,128]{2,1,0:T(8,128)(2,1)S(1)} async-done(((bf16[16,32,128]{2,1,0:T(8,128)(2,1)}), bf16[16,32,128]{2,1,0:T(8,128)(2,1)S(1)}, u32[]{:S(2)}, u32[]{:S(2)}) %all-to-all-start.1) | async-done | bytes 131104 | tf_op jit(solution)/shard_map/all_to_all | solution.py:234
  82.5 0.0 copy-done.4
  82.5 0.0 copy-done.5
  82.5 0.0 copy-done.6
  82.5 0.8 last.3
  (2 shorter events, 0.0 us)
Async XLA Ops:
  0.6 16.9 %copy-start = (bf16[2,256,256]{2,1,0:T(8,128)(2,1)S(1)}, bf16[2,256,256]{2,1,0:T(8,128)(2,1)}, u32[]{:S(2)}) copy-start(bf16[2,256,256]{2,1,0:T(8,128)(2,1)} %constant.15.clone.wide) | copy-start | bytes 786436
  0.6 16.9 %copy-start.3 = (bf16[2,128,256]{2,1,0:T(8,128)(2,1)S(1)}, bf16[2,128,256]{2,1,0:T(8,128)(2,1)}, u32[]{:S(2)}) copy-start(bf16[2,128,256]{2,1,0:T(8,128)(2,1)} %constant.16.clone.last) | copy-start | bytes 393220
  2.5 15.0 %copy-start.1 = (f32[2,128,128]{2,1,0:T(8,128)S(1)}, f32[2,128,128]{2,1,0:T(8,128)}, u32[]{:S(2)}) copy-start(f32[2,128,128]{2,1,0:T(8,128)} %constant.17.clone.twiddle) | copy-start | bytes 393220
  2.5 15.0 %copy-start.2 = (bf16[256,256]{1,0:T(8,128)(2,1)S(1)}, bf16[256,256]{1,0:T(8,128)(2,1)}, u32[]{:S(2)}) copy-start(bf16[256,256]{1,0:T(8,128)(2,1)} %constant.14.clone.first) | copy-start | bytes 393220
  2.5 15.0 %all-to-all-start = ((bf16[16,32,128]{2,1,0:T(8,128)(2,1)}), bf16[16,32,128]{2,1,0:T(8,128)(2,1)S(1)}, u32[]{:S(2)}, u32[]{:S(2)}) async-start(bf16[16,32,128]{2,1,0:T(8,128)(2,1)} %bitcast.1), calls=%async_computation | async-start | bytes 262144 | tf_op jit(solution)/shard_map/all_to_all | solution.py:234
  18.8 49.6 %collective-permute-start = (bf16[2,16,16,128]{3,2,1,0:T(8,128)(2,1)S(1)}, bf16[2,16,16,128]{3,2,1,0:T(8,128)(2,1)S(1)}, u32[]{:S(2)}, u32[]{:S(2)}) collective-permute-start(bf16[2,16,16,128]{3,2,1,0:T(8,128)(2,1)S(1)} %get-tuple-element.16), channel_id=1, source_target_pairs={{0,512},{512,0},{1,513},{513,1},{2,514},{514,2},{3,515},{515,3},{4... | collective-permute-start | bytes 393224 | tf_op jit(solution)/shard_map/ppermute | solution.py:253
  70.8 11.7 %all-to-all-start.1 = ((bf16[16,32,128]{2,1,0:T(8,128)(2,1)}), bf16[16,32,128]{2,1,0:T(8,128)(2,1)S(1)}, u32[]{:S(2)}, u32[]{:S(2)}) async-start(bf16[16,32,128]{2,1,0:T(8,128)(2,1)} %bitcast.3), calls=%async_computation.1 | async-start | bytes 262144 | tf_op jit(solution)/shard_map/all_to_all | solution.py:234
  74.6 7.8 %copy-start.4 = (bf16[128,256]{1,0:T(8,128)(2,1)S(1)}, bf16[128,256]{1,0:T(8,128)(2,1)}, u32[]{:S(2)}) copy-start(bf16[128,256]{1,0:T(8,128)(2,1)} %key_in.3) | copy-start | bytes 196612
  74.6 7.8 %copy-start.5 = (bf16[128,256]{1,0:T(8,128)(2,1)S(1)}, bf16[128,256]{1,0:T(8,128)(2,1)}, u32[]{:S(2)}) copy-start(bf16[128,256]{1,0:T(8,128)(2,1)} %value.3) | copy-start | bytes 196612
  74.6 7.8 %copy-start.6 = (bf16[128,256]{1,0:T(8,128)(2,1)S(1)}, bf16[128,256]{1,0:T(8,128)(2,1)}, u32[]{:S(2)}) copy-start(bf16[128,256]{1,0:T(8,128)(2,1)} %out_grad.3) | copy-start | bytes 196612
